TPU v7x, 256 devices: a whole 4x4x8 slice. The times are simulated.
256 devices in a mesh: worker: 16 (over x_lo, y, core), shard: 16 (over z, x_hi).
Axes of the slice: x: 4 (x_hi: 2, x_lo: 2; x = x_hi * 2 + x_lo), y: 4, z: 8, core: 2. Of those that a mesh axis runs over, the one named last changes fastest.
Arguments:
- momentum: float32 [16, 8388608], P('worker', 'shard'), may hold values from -6 to 6
- gradient: float32 [16, 8388608], P('worker', 'shard'), may hold values from -40 to 40
- weights: float32 [8388608], P('shard'), may hold values from -0.6 to 0.6
Outputs:
- new_momentum: float32 [16, 8388608], P('worker', 'shard')
- new_weights: float32 [8388608], P('shard')
All inputs are finite; a program needn't handle non-finite values.
Results may differ from a plain program's by a relative error of at most 0.0003.
Values sent between devices are 32-bit elements; how exact they have to be, the bound alone decides.
A program may use at most 64 MiB of HBM per device.

v0:
```python
import jax
import jax.numpy as jnp
from jax import lax
from jax.sharding import PartitionSpec as P


def sent_to_all(value, axis):
    length = lax.axis_size(axis)
    return lax.all_to_all(
        jnp.broadcast_to(value[None], (length, *value.shape)), axis, 0, 0, tiled=True
    )


def in_order(blocks, dim):
    blocks = jnp.moveaxis(blocks, 0, dim)
    lengths = blocks.shape
    return blocks.reshape(*lengths[:dim], lengths[dim] * lengths[dim + 1], *lengths[dim + 2 :])


def gather_directly(value, axis, dim):
    blocks = sent_to_all(value, axis)
    return in_order(blocks, dim)


def order_pairs(stacked):
    former = stacked[0::2]
    latter = stacked[1::2]
    paired = jnp.stack([jnp.minimum(former, latter), jnp.maximum(former, latter)], 1)
    return paired.reshape(stacked.shape)


def trimmed_mean(values):
    members = values.shape[0]
    trim_count = members // 4

    def one_round(step_index, current):
        current = order_pairs(current)
        middle = order_pairs(current[1 : members - 1])
        return jnp.concatenate([current[:1], middle, current[members - 1 :]], 0)

    ordered = lax.fori_loop(0, members // 2, one_round, values)
    kept = ordered[trim_count : members - trim_count]
    return jnp.sum(kept, axis=0) / (members - 2 * trim_count)


def body(momentum, gradient, weights):
    updated = 0.9 * momentum + gradient
    shard_len = updated.shape[1]
    workers_here = lax.axis_size("worker")
    block_len = shard_len // workers_here
    blocks = updated.reshape(workers_here, block_len // 128, 128)
    trimmed = trimmed_mean(
        lax.all_to_all(blocks, "worker", split_axis=0, concat_axis=0, tiled=True)
    )
    start = lax.axis_index("worker") * block_len
    own_weights = lax.dynamic_slice_in_dim(weights, start, block_len)
    own_new = own_weights - 0.1 * trimmed.reshape(block_len)
    new_weights = gather_directly(own_new, "worker", 0)
    return (updated, new_weights)


def solution(mesh):
    return jax.shard_map(
        body,
        mesh=mesh,
        in_specs=(P("worker", "shard"), P("worker", "shard"), P("shard")),
        out_specs=(P("worker", "shard"), P("shard")),
        check_vma=False,
    )
```

profile of v0, /device:TPU:1, one launch (start us, length us, event | category | flops | bytes accessed | tf_op | source)
XLA Modules:
  0.0 88.5 jit_solution(5776479268664922054)
XLA Ops:
  0.6 5.7 %multiply_add_fusion = f32[1,524288]{1,0:T(1,128)} fusion(f32[1,524288]{1,0:T(1,128)} %param.6, f32[1,524288]{1,0:T(1,128)} %param.5), kind=kLoop, calls=%fused_computation.7 | loop fusion | flops 1048576 | bytes 6291456 | tf_op jit(solution)/shard_map/add | solution.py:47
  6.3 6.9 %all-to-all-start = ((f32[16,256,128]{2,1,0:T(8,128)}), f32[16,256,128]{2,1,0:T(8,128)S(1)}, u32[]{:S(2)}, u32[]{:S(2)}) async-start(f32[16,256,128]{2,1,0:T(8,128)} %bitcast.25), calls=%async_computation | async-start | bytes 4194304 | tf_op jit(solution)/shard_map/all_to_all | solution.py:53
  13.2 27.6 %all-to-all-done = f32[16,256,128]{2,1,0:T(8,128)S(1)} async-done(((f32[16,256,128]{2,1,0:T(8,128)}), f32[16,256,128]{2,1,0:T(8,128)S(1)}, u32[]{:S(2)}, u32[]{:S(2)}) %all-to-all-start) | async-done | bytes 2097184 | tf_op jit(solution)/shard_map/all_to_all | solution.py:53
  40.8 11.0 %while.10 = (s32[]{:T(128)}, f32[16,256,128]{2,1,0:T(8,128)S(1)}, s32[]{:T(128)}) while((s32[]{:T(128)}, f32[16,256,128]{2,1,0:T(8,128)S(1)}, s32[]{:T(128)}) %tuple.31), condition=%wide.region_1.0_spmd, body=%wide.region_0.0_spmd.sunk | while | flops 3014658 | bytes 31981612 | solution.py:41
  40.8 0.2 minimum_bitcast_fusion.4
  41.0 0.2 pad_maximum_fusion.6
  41.2 0.2 copy.10
  41.5 0.1 minimum_bitcast_fusion.5
  42.0 0.2 pad_maximum_fusion.8
  42.2 0.2 minimum_bitcast_fusion.4
  42.4 0.2 pad_maximum_fusion.6
  42.6 0.2 copy.10
  42.9 0.1 minimum_bitcast_fusion.5
  43.3 0.2 pad_maximum_fusion.8
  43.6 0.2 minimum_bitcast_fusion.4
  43.7 0.2 pad_maximum_fusion.6
  43.9 0.2 copy.10
  44.3 0.1 minimum_bitcast_fusion.5
  44.7 0.2 pad_maximum_fusion.8
  44.9 0.2 minimum_bitcast_fusion.4
  45.1 0.2 pad_maximum_fusion.6
  45.3 0.2 copy.10
  45.7 0.1 minimum_bitcast_fusion.5
  46.1 0.2 pad_maximum_fusion.8
  46.3 0.2 minimum_bitcast_fusion.4
  46.5 0.2 pad_maximum_fusion.6
  46.7 0.2 copy.10
  47.1 0.1 minimum_bitcast_fusion.5
  47.5 0.2 pad_maximum_fusion.8
  47.7 0.2 minimum_bitcast_fusion.4
  47.9 0.2 pad_maximum_fusion.6
  48.1 0.2 copy.10
  48.4 0.1 minimum_bitcast_fusion.5
  48.9 0.2 pad_maximum_fusion.8
  49.1 0.2 minimum_bitcast_fusion.4
  49.3 0.2 pad_maximum_fusion.6
  49.5 0.2 copy.10
  49.8 0.1 minimum_bitcast_fusion.5
  50.3 0.2 pad_maximum_fusion.8
  50.5 0.2 minimum_bitcast_fusion.4
  50.7 0.2 pad_maximum_fusion.6
  50.8 0.2 copy.10
  51.2 0.1 minimum_bitcast_fusion.5
  51.6 0.2 pad_maximum_fusion.8
  51.9 0.9 %bitcast_subtract_fusion = f32[32768]{0:T(1024)S(1)} fusion(f32[256,128]{1,0:T(8,128)S(1)} %slice_reduce_fusion, f32[524288]{0:T(1024)} %param.7, s32[]{:T(128)S(6)} %select_n.3), kind=kLoop, calls=%fused_computation.9 | loop fusion | flops 65536 | bytes 393220 | tf_op jit(solution)/shard_map/sub | solution.py:57
  52.8 1.6 %broadcast_in_dim.2 = f32[16,1,32768]{2,1,0:T(1,128)S(1)} broadcast(f32[32768]{0:T(1024)S(1)} %bitcast_subtract_fusion), dimensions={2} | broadcast | bytes 2228224 | tf_op jit(solution)/shard_map/broadcast_in_dim | solution.py:10
  54.5 32.6 %all_to_all.11 = f32[16,1,32768]{2,1,0:T(1,128)S(1)} all-to-all(f32[16,1,32768]{2,1,0:T(1,128)S(1)} %broadcast_in_dim.2), channel_id=1, replica_groups=mesh['worker'=16,'shard'=16] {'worker'}, dimensions={0} | all-to-all | bytes 4194304 | tf_op jit(solution)/shard_map/all_to_all | solution.py:9
  87.0 1.5 %copy.20 = f32[524288]{0:T(1024)} copy(f32[524288]{0:T(1024)S(1)} %bitcast.26) | data formatting | bytes 4194304
  (33 shorter events, 3.4 us)
Async XLA Ops:
  6.3 34.5 %all-to-all-start = ((f32[16,256,128]{2,1,0:T(8,128)}), f32[16,256,128]{2,1,0:T(8,128)S(1)}, u32[]{:S(2)}, u32[]{:S(2)}) async-start(f32[16,256,128]{2,1,0:T(8,128)} %bitcast.25), calls=%async_computation | async-start | bytes 4194304 | tf_op jit(solution)/shard_map/all_to_all | solution.py:53
where the time goes:
time: 88.7 us; the launch traced here: 88.5 us
  blocking collectives  32.6 us (37%)
  waiting for transfers between devices  27.6 us (31%)
  other arithmetic  13.2 us (15%)
  local copies, waits for them, and re-layouts  6.91 us (8%)
  starting transfers between devices  6.9 us (8%)
    all_to_all x1, blocking collectives, sent_to_all(): lax.all_to_all(jnp.broadcast_to(value[None], (length, *value.shape)), axi...  32.6 us
    all_to_all x1, waiting for transfers between devices, body(): lax.all_to_all(blocks, 'worker', split_axis=0, concat_axis=0, tiled=True)  27.6 us
    all_to_all x1, starting transfers between devices, body(): lax.all_to_all(blocks, 'worker', split_axis=0, concat_axis=0, tiled=True)  6.9 us
    add x1, other arithmetic, body(): updated = 0.9 * momentum + gradient  5.66 us
    another operation x32, other arithmetic, order_pairs(): jnp.stack([jnp.minimum(former, latter), jnp.maximum(former, latter)], 1)  5.08 us
    another operation x16, local copies, waits for them, and re-layouts, order_pairs(): jnp.stack([jnp.minimum(former, latter), jnp.maximum(former, latter)], 1)  2.59 us
  transfers between devices with their start and end apart: 1, of which 1 were waited for; matrix products, arithmetic and copies ran while one was open for 0% of the time, Pallas kernels for 0%

commit v1 on v0

v1 whole, which is shorter than its diff:
```python
import functools

import jax
import jax.numpy as jnp
from jax import lax
from jax.experimental import pallas as pl
from jax.experimental.pallas import tpu as pltpu
from jax.sharding import PartitionSpec as P

MESH = pl.DeviceIdType.MESH
LANES = 128
N = 16
CHUNKS = (64, 64, 64, 64)
VIA_X = (False, True, False, False)
SORT8 = (
    ((0, 2), (1, 3), (4, 6), (5, 7)),
    ((0, 4), (1, 5), (2, 6), (3, 7)),
    ((0, 1), (2, 3), (4, 5), (6, 7)),
    ((2, 4), (3, 5)),
    ((1, 4), (3, 6)),
    ((1, 2), (3, 4), (5, 6)),
)


def sort8(values):
    values = list(values)
    for layer in SORT8:
        for i, j in layer:
            a, b = values[i], values[j]
            values[i], values[j] = jnp.minimum(a, b), jnp.maximum(a, b)
    return values


def trimmed_sum(values):
    a, b = sort8(values[:8]), sort8(values[8:])
    kept = [jnp.maximum(a[i], b[3 - i]) for i in range(4)]
    kept += [jnp.minimum(a[4 + i], b[7 - i]) for i in range(4)]
    while len(kept) > 1:
        kept = [kept[i] + kept[i + 1] for i in range(0, len(kept), 2)]
    return kept[0]


def exchange(m_ref, g_ref, w_ref, upd, new_w, m_buf, g_buf, w_buf, recv,
             load_sem, w_sem, out_sem, in_sem, near_sem, far_sem, core_sem, gather_sem):
    me = lax.axis_index("worker")
    x, y, c = me // 8, (me // 2) % 4, me % 2

    def at(dx, dy, dc):
        return ((x + dx) % 2) * 8 + ((y + dy) % 4) * 2 + (c + dc) % 2

    def wait_bytes(ref, sem):
        pltpu.make_async_copy(ref, ref, sem).wait()

    def send(src, dst, s_sem, r_sem, peer):
        pltpu.make_async_remote_copy(
            src_ref=src, dst_ref=dst, send_sem=s_sem, recv_sem=r_sem,
            device_id={"worker": peer}, device_id_type=MESH,
        ).start()

    offsets = [(dx, dy, dc) for dy in (2, 1, 3, 0) for dx in (1, 0) for dc in (0, 1)]
    offsets = [o for o in offsets if o != (0, 0, 0)]
    starts = [sum(CHUNKS[:k]) for k in range(len(CHUNKS))]
    spans = [pl.ds(s, r) for s, r in zip(starts, CHUNKS)]

    barrier = pltpu.get_barrier_semaphore()
    for o in offsets:
        pl.semaphore_signal(barrier, inc=1, device_id={"worker": at(*o)}, device_id_type=MESH)
    loads = []
    for k, span in enumerate(spans):
        pair = (
            pltpu.make_async_copy(m_ref.at[:, span], m_buf.at[:, span], load_sem.at[0, k]),
            pltpu.make_async_copy(g_ref.at[:, span], g_buf.at[:, span], load_sem.at[1, k]),
        )
        for copy in pair:
            copy.start()
        loads.append(pair)
    w_load = pltpu.make_async_copy(w_ref.at[me], w_buf, w_sem)
    w_load.start()

    def update(k):
        for copy in loads[k]:
            copy.wait()

        def one(d, _):
            upd[d, spans[k], :] = 0.9 * m_buf[d, spans[k], :] + g_buf[d, spans[k], :]
            return 0

        lax.fori_loop(0, N, one, 0)
        recv[me, spans[k], :] = upd[me, spans[k], :]

    def scatter(k):
        for o in offsets:
            peer = at(*o)
            send(upd.at[peer, spans[k]], recv.at[me, spans[k]], out_sem.at[k], in_sem.at[k], peer)

    update(0)
    for k in range(len(CHUNKS)):
        if k + 1 < len(CHUNKS):
            update(k + 1)
        if k == 0:
            pl.semaphore_wait(barrier, len(offsets))
        scatter(k)
    w_load.wait()

    def gather(block, k, r_sem, peer):
        send(new_w.at[block, spans[k]], new_w.at[block, spans[k]], gather_sem.at[k], r_sem, peer)

    other_core, other_x = at(0, 0, 1), at(1, 0, 0)
    for k in range(len(CHUNKS)):
        wait_bytes(recv.at[pl.ds(0, N - 1), spans[k]], in_sem.at[k])

        def one(r, _, k=k):
            rows = pl.ds(pl.multiple_of(starts[k] + r * 8, 8), 8)
            total = trimmed_sum([recv[d, rows, :] for d in range(N)])
            new_w[me, rows, :] = w_buf[rows, :] - 0.1 * (total * 0.125)
            return 0

        lax.fori_loop(0, CHUNKS[k] // 8, one, 0)
        gather(me, k, near_sem.at[k, 0], other_x)
        for i, dy in enumerate((2, 1, 3)):
            gather(me, k, near_sem.at[k, i + 1], at(0, dy, 0))
        gather(me, k, core_sem, other_core)

    for k in range(len(CHUNKS)):
        wait_bytes(new_w.at[other_x, spans[k]], near_sem.at[k, 0])
        if not VIA_X[k]:
            gather(other_x, k, far_sem.at[k, 1], at(0, 1, 0))
            gather(other_x, k, far_sem.at[k, 2], at(0, 3, 0))
        gather(other_x, k, core_sem, other_core)
        for i, dy in enumerate((2, 1, 3)):
            block = at(0, -dy, 0)
            wait_bytes(new_w.at[block, spans[k]], near_sem.at[k, i + 1])
            if dy == 2 or VIA_X[k]:
                gather(block, k, far_sem.at[k, i], other_x)
            gather(block, k, core_sem, other_core)
    for k in range(len(CHUNKS)):
        for i, dy in enumerate((2, 1, 3)):
            block = at(1, -dy, 0)
            wait_bytes(new_w.at[block, spans[k]], far_sem.at[k, i])
            gather(block, k, core_sem, other_core)
    wait_bytes(new_w.at[pl.ds(0, 8)], core_sem)
    for k in range(len(CHUNKS)):
        wait_bytes(recv.at[pl.ds(0, N - 1), spans[k]], out_sem.at[k])
        wait_bytes(recv.at[pl.ds(0, N - 1), spans[k]], gather_sem.at[k])


def put_out(upd, new_w, upd_out, new_w_out, sems):
    parts = 4
    copies = []
    for i, (src, dst) in enumerate(((upd, upd_out), (new_w, new_w_out))):
        for p in range(parts):
            span = pl.ds(p * (N // parts), N // parts)
            copies.append(pltpu.make_async_copy(src.at[span], dst.at[span], sems.at[i, p]))
    for copy in copies:
        copy.start()
    for copy in copies:
        copy.wait()


def body(momentum, gradient, weights):
    rows = momentum.shape[1] // (N * LANES)
    shape = (N, rows, LANES)
    k = len(CHUNKS)
    any_spec = pl.BlockSpec(memory_space=pl.ANY)
    upd, new_w = pl.pallas_call(
        exchange,
        out_shape=(pltpu.VMEM(shape, jnp.float32), pltpu.VMEM(shape, jnp.float32)),
        in_specs=[pl.BlockSpec(memory_space=pltpu.HBM)] * 3,
        out_specs=(pl.BlockSpec(memory_space=pltpu.VMEM),) * 2,
        scratch_shapes=[
            pltpu.VMEM(shape, jnp.float32),
            pltpu.VMEM(shape, jnp.float32),
            pltpu.VMEM(shape[1:], jnp.float32),
            pltpu.VMEM(shape, jnp.float32),
            pltpu.SemaphoreType.DMA((2, k)),
            pltpu.SemaphoreType.DMA,
            pltpu.SemaphoreType.DMA((k,)),
            pltpu.SemaphoreType.DMA((k,)),
            pltpu.SemaphoreType.DMA((k, 4)),
            pltpu.SemaphoreType.DMA((k, 3)),
            pltpu.SemaphoreType.DMA,
            pltpu.SemaphoreType.DMA((k,)),
        ],
        compiler_params=pltpu.CompilerParams(
            collective_id=0, has_side_effects=True, vmem_limit_bytes=16 << 20
        ),
        name="exchange",
    )(*(pltpu.with_memory_space_constraint(a.reshape(shape), pltpu.HBM) for a in (momentum, gradient, weights)))
    upd_out, new_w_out = pl.pallas_call(
        put_out,
        out_shape=(jax.ShapeDtypeStruct(shape, jnp.float32),) * 2,
        in_specs=[any_spec] * 2,
        out_specs=(any_spec, any_spec),
        scratch_shapes=[pltpu.SemaphoreType.DMA((2, 4))],
        compiler_params=pltpu.CompilerParams(vmem_limit_bytes=1 << 20),
        name="put_out",
    )(upd, new_w)
    return upd_out.reshape(momentum.shape), new_w_out.reshape(weights.shape)


def solution(mesh):
    return jax.shard_map(
        body,
        mesh=mesh,
        in_specs=(P("worker", "shard"), P("worker", "shard"), P("shard")),
        out_specs=(P("worker", "shard"), P("shard")),
        check_vma=False,
    )
```

time: 88.7 us -> 43.4 us (0.49)
  Pallas kernels: 0 us -> 42.7 us
  blocking collectives: 32.6 us -> 0 us
  waiting for transfers between devices: 27.6 us -> 0 us
  other arithmetic: 13.2 us -> 0 us
  local copies, waits for them, and re-layouts: 6.91 us -> 0 us
  starting transfers between devices: 6.9 us -> 0 us
    pallas_call x0 -> x2, Pallas kernels: none -> 42.7 us  [the longest x1 40.6 us: body(): pl.pallas_call(exchange, out_shape=(pltpu.VMEM(shape, jnp.float32), pltpu...]
    all_to_all x1 -> x0, blocking collectives: 32.6 us -> none  [sent_to_all(): lax.all_to_all(jnp.broadcast_to(value[None], (length, *value.shape)), axi...]
    all_to_all x1 -> x0, waiting for transfers between devices: 27.6 us -> none  [body(): lax.all_to_all(blocks, 'worker', split_axis=0, concat_axis=0, tiled=True)]
    all_to_all x1 -> x0, starting transfers between devices: 6.9 us -> none  [body(): lax.all_to_all(blocks, 'worker', split_axis=0, concat_axis=0, tiled=True)]
    add x1 -> x0, other arithmetic: 5.66 us -> none  [body(): updated = 0.9 * momentum + gradient]
    another operation x32 -> x0, other arithmetic: 5.08 us -> none  [order_pairs(): jnp.stack([jnp.minimum(former, latter), jnp.maximum(former, latter)], 1)]
    another operation x16 -> x0, local copies, waits for them, and re-layouts: 2.59 us -> none  [order_pairs(): jnp.stack([jnp.minimum(former, latter), jnp.maximum(former, latter)], 1)]
    broadcast_in_dim x1 -> x0, local copies, waits for them, and re-layouts: 1.61 us -> none  [sent_to_all(): jnp.broadcast_to(value[None], (length, *value.shape))]
  transfers between devices with their start and end apart: 1 -> 0, of which waited for: 1 -> 0; matrix products, arithmetic and copies ran while one was open for 0% -> 0% of each run, Pallas kernels for 0% -> 0%
where the time goes in v1:
time: 43.4 us; the launch traced here: 43.3 us
  Pallas kernels  42.7 us (98%)
  between operations  0.64 us (1%)
    pallas_call x1, Pallas kernels, body(): pl.pallas_call(exchange, out_shape=(pltpu.VMEM(shape, jnp.float32), pltpu...  40.6 us
    pallas_call x1, Pallas kernels, body(): pl.pallas_call(put_out, out_shape=(jax.ShapeDtypeStruct(shape, jnp.float3...  2.07 us

profile of v1, /device:TPU:1, one launch (start us, length us, event | category | flops | bytes accessed | tf_op | source)
XLA Modules:
  0.0 43.3 jit_solution(17255570045871783508)
XLA Ops:
  0.6 40.6 %exchange.1 = (f32[16,256,128]{2,1,0:T(8,128)S(1)}, f32[16,256,128]{2,1,0:T(8,128)S(1)}) custom-call(f32[16,256,128]{2,1,0:T(8,128)} %bitcast.5, f32[16,256,128]{2,1,0:T(8,128)} %bitcast.6, f32[16,256,128]{2,1,0:T(8,128)} %bitcast.7), custom_call_target="tpu_custom_call" | custom-call | tf_op jit(solution)/shard_map/exchange/pallas_call | solution.py:165
  41.3 2.1 %put_out.1 = (f32[16,256,128]{2,1,0:T(8,128)}, f32[16,256,128]{2,1,0:T(8,128)}) custom-call(f32[16,256,128]{2,1,0:T(8,128)S(1)} %get-tuple-element.6.upd, f32[16,256,128]{2,1,0:T(8,128)S(1)} %get-tuple-element.7.new_w), custom_call_target="tpu_custom_call" | custom-call | tf_op jit(solution)/shard_map/put_out/pallas_call | solution.py:189

commit v2 on v1

v2 whole, which is shorter than its diff:
```python
import functools

import jax
import jax.numpy as jnp
from jax import lax
from jax.experimental import pallas as pl
from jax.experimental.pallas import tpu as pltpu
from jax.sharding import PartitionSpec as P

MESH = pl.DeviceIdType.MESH
LANES = 128
N = 16
CHUNKS = (64, 64, 64, 64)
NEARS = 2
ROUTES = "xyyY"
STEP = 128
SORT8 = (
    ((0, 2), (1, 3), (4, 6), (5, 7)),
    ((0, 4), (1, 5), (2, 6), (3, 7)),
    ((0, 1), (2, 3), (4, 5), (6, 7)),
    ((2, 4), (3, 5)),
    ((1, 4), (3, 6)),
    ((1, 2), (3, 4), (5, 6)),
)


def sort8(values):
    values = list(values)
    for layer in SORT8:
        for i, j in layer:
            a, b = values[i], values[j]
            values[i], values[j] = jnp.minimum(a, b), jnp.maximum(a, b)
    return values


def trimmed_sum(values):
    a, b = sort8(values[:8]), sort8(values[8:])
    kept = [jnp.maximum(a[i], b[3 - i]) for i in range(4)]
    kept += [jnp.minimum(a[4 + i], b[7 - i]) for i in range(4)]
    while len(kept) > 1:
        kept = [kept[i] + kept[i + 1] for i in range(0, len(kept), 2)]
    return kept[0]


def exchange(m_ref, g_ref, w_ref, upd, new_w, m_buf, g_buf, w_buf, recv,
             round_sem, load_sem, w_sem, out_sem, in_sem, near_sem, far_sem, core_sem, gather_sem):
    me = lax.axis_index("worker")
    x, y, c = me // 8, (me // 2) % 4, me % 2

    def at(dx, dy, dc):
        return ((x + dx) % 2) * 8 + ((y + dy) % 4) * 2 + (c + dc) % 2

    def wait_bytes(ref, sem):
        pltpu.make_async_copy(ref, ref, sem).wait()

    def send(src, dst, s_sem, r_sem, peer):
        pltpu.make_async_remote_copy(
            src_ref=src, dst_ref=dst, send_sem=s_sem, recv_sem=r_sem,
            device_id={"worker": peer}, device_id_type=MESH,
        ).start()

    near = [(1, 0, 0), (1, 0, 1), (0, 1, 0), (0, 3, 0), (0, 1, 1), (0, 3, 1), (0, 0, 1)]
    middle = [(0, 2, 0), (0, 2, 1), (1, 1, 0), (1, 3, 0), (1, 1, 1), (1, 3, 1)]
    last = [(1, 2, 0), (1, 2, 1)]
    ring = [(1, 0, 0), (0, 1, 0), (0, 3, 0)]
    starts = [sum(CHUNKS[:k]) for k in range(len(CHUNKS))]
    spans = [pl.ds(s, r) for s, r in zip(starts, CHUNKS)]
    every = range(len(CHUNKS))

    def signal(sem, o):
        pl.semaphore_signal(sem, inc=1, device_id={"worker": at(*o)}, device_id_type=MESH)

    barrier = pltpu.get_barrier_semaphore()
    for o in near:
        signal(barrier, o)
    order = near + middle + last + [(0, 0, 0)]
    loads = []
    for i, o in enumerate(order):
        block = at(*o)
        pair = (
            pltpu.make_async_copy(m_ref.at[block], m_buf.at[block], load_sem.at[0, i]),
            pltpu.make_async_copy(g_ref.at[block], g_buf.at[block], load_sem.at[1, i]),
        )
        for copy in pair:
            copy.start()
        loads.append(pair)
    w_load = pltpu.make_async_copy(w_ref.at[me], w_buf, w_sem)
    w_load.start()

    def update(i):
        for copy in loads[i]:
            copy.wait()
        block = at(*order[i])

        def one(r, _):
            rows = pl.ds(pl.multiple_of(r * STEP, STEP), STEP)
            upd[block, rows, :] = 0.9 * m_buf[block, rows, :] + g_buf[block, rows, :]
            return 0

        lax.fori_loop(0, upd.shape[1] // STEP, one, 0)

    def scatter(i, k):
        peer = at(*order[i])
        send(upd.at[peer, spans[k]], recv.at[me, spans[k]], out_sem, in_sem.at[k], peer)

    first, second = len(near), len(near) + len(middle)
    update(0)
    for i in range(first):
        update(i + 1)
        if i == 0:
            pl.semaphore_wait(barrier, len(near))
            for o in ring:
                signal(round_sem.at[0], o)
        scatter(i, 0)
    for k in range(1, NEARS):
        for i in range(first):
            scatter(i, k)
    pl.semaphore_wait(round_sem.at[0], len(ring))
    for o in ring:
        signal(round_sem.at[1], o)
    for i in range(first + 1, second + 1):
        update(i)
        scatter(i - 1, 0)
    for i in range(second + 1, len(order)):
        update(i)
    pl.semaphore_wait(round_sem.at[1], len(ring))
    for i in range(second, len(order) - 1):
        scatter(i, 0)
    for k in every[1:]:
        for i in reversed(range(first if k < NEARS else 0, len(order) - 1)):
            scatter(i, k)

    def own(r, _):
        rows = pl.ds(pl.multiple_of(r * 32, 32), 32)
        recv[me, rows, :] = upd[me, rows, :]
        return 0

    lax.fori_loop(0, upd.shape[1] // 32, own, 0)
    w_load.wait()

    other_core, other_x = at(0, 0, 1), at(1, 0, 0)

    sides = ((1, 1), (2, 3))

    def gather(block, k, r_sem, peer):
        part = new_w.at[block, spans[k]]
        send(part, part, gather_sem, r_sem, peer)

    def select(k):
        wait_bytes(recv.at[pl.ds(0, N - 1), spans[k]], in_sem.at[k])

        def one(r, _):
            rows = pl.ds(pl.multiple_of(starts[k] + r * 8, 8), 8)
            total = trimmed_sum([recv[d, rows, :] for d in range(N)])
            new_w[me, rows, :] = w_buf[rows, :] - 0.1 * (total * 0.125)
            return 0

        lax.fori_loop(0, CHUNKS[k] // 8, one, 0)
        gather(me, k, near_sem.at[k, 3], at(0, 2, 0))
        for i, dy in sides:
            gather(me, k, near_sem.at[k, i], at(0, dy, 0))
        gather(me, k, near_sem.at[k, 0], other_x)
        gather(me, k, core_sem, other_core)

    def relay(k):
        wait_bytes(new_w.at[other_x, spans[k]], near_sem.at[k, 0])
        if ROUTES[k] != "x":
            for i, dy in sides:
                gather(other_x, k, far_sem.at[k, i], at(0, dy, 0))
                if ROUTES[k] == "Y":
                    gather(other_x, k, core_sem, at(0, dy, 1))
        gather(other_x, k, core_sem, other_core)
        for i, dy in sides:
            block = at(0, -dy, 0)
            wait_bytes(new_w.at[block, spans[k]], near_sem.at[k, i])
            if ROUTES[k] == "x":
                gather(block, k, far_sem.at[k, i], other_x)
            gather(block, k, core_sem, other_core)
        block = at(0, 2, 0)
        wait_bytes(new_w.at[block, spans[k]], near_sem.at[k, 3])
        gather(block, k, far_sem.at[k, 0], other_x)
        if ROUTES[k] == "Y":
            gather(block, k, core_sem, at(1, 0, 1))
        gather(block, k, core_sem, other_core)

    def relay_far(k):
        for i, dy in (*sides, (0, 2)):
            block = at(1, -dy, 0)
            wait_bytes(new_w.at[block, spans[k]], far_sem.at[k, i])
            if ROUTES[k] != "Y":
                gather(block, k, core_sem, other_core)

    for step in (select, relay, relay_far):
        for k in every:
            step(k)
    wait_bytes(new_w.at[pl.ds(0, 8)], core_sem)
    wait_bytes(recv.at[pl.ds(0, N - 1)], out_sem)
    wait_bytes(recv.at[pl.ds(0, N - 1)], gather_sem)


def put_out(upd, new_w, upd_out, new_w_out, sems):
    parts = sems.shape[1]
    copies = []
    for i, (src, dst) in enumerate(((upd, upd_out), (new_w, new_w_out))):
        for p in range(parts):
            span = pl.ds(p * (N // parts), N // parts)
            copies.append(pltpu.make_async_copy(src.at[span], dst.at[span], sems.at[i, p]))
    for copy in copies:
        copy.start()
    for copy in copies:
        copy.wait()


def body(momentum, gradient, weights):
    rows = momentum.shape[1] // (N * LANES)
    shape = (N, rows, LANES)
    k = len(CHUNKS)
    any_spec = pl.BlockSpec(memory_space=pl.ANY)
    upd, new_w = pl.pallas_call(
        exchange,
        out_shape=(pltpu.VMEM(shape, jnp.float32), pltpu.VMEM(shape, jnp.float32)),
        in_specs=[pl.BlockSpec(memory_space=pltpu.HBM)] * 3,
        out_specs=(pl.BlockSpec(memory_space=pltpu.VMEM),) * 2,
        scratch_shapes=[
            pltpu.VMEM(shape, jnp.float32),
            pltpu.VMEM(shape, jnp.float32),
            pltpu.VMEM(shape[1:], jnp.float32),
            pltpu.VMEM(shape, jnp.float32),
            pltpu.SemaphoreType.REGULAR((2,)),
            pltpu.SemaphoreType.DMA((2, N)),
            pltpu.SemaphoreType.DMA,
            pltpu.SemaphoreType.DMA,
            pltpu.SemaphoreType.DMA((k,)),
            pltpu.SemaphoreType.DMA((k, 4)),
            pltpu.SemaphoreType.DMA((k, 3)),
            pltpu.SemaphoreType.DMA,
            pltpu.SemaphoreType.DMA,
        ],
        compiler_params=pltpu.CompilerParams(
            collective_id=0, has_side_effects=True, vmem_limit_bytes=16 << 20
        ),
        name="exchange",
    )(*(pltpu.with_memory_space_constraint(a.reshape(shape), pltpu.HBM) for a in (momentum, gradient, weights)))
    upd_out, new_w_out = pl.pallas_call(
        put_out,
        out_shape=(jax.ShapeDtypeStruct(shape, jnp.float32),) * 2,
        in_specs=[any_spec] * 2,
        out_specs=(any_spec, any_spec),
        scratch_shapes=[pltpu.SemaphoreType.DMA((2, 1))],
        compiler_params=pltpu.CompilerParams(vmem_limit_bytes=1 << 20),
        name="put_out",
    )(upd, new_w)
    return upd_out.reshape(momentum.shape), new_w_out.reshape(weights.shape)


def solution(mesh):
    return jax.shard_map(
        body,
        mesh=mesh,
        in_specs=(P("worker", "shard"), P("worker", "shard"), P("shard")),
        out_specs=(P("worker", "shard"), P("shard")),
        check_vma=False,
    )
```

time: 43.4 us -> 42.1 us (0.970)
  Pallas kernels: 42.7 us -> 41.4 us
    pallas_call x1, Pallas kernels: 40.6 us -> 39.4 us  [body(): pl.pallas_call(exchange, out_shape=(pltpu.VMEM(shape, jnp.float32), pltpu...]
where the time goes in v2:
time: 42.1 us; the launch traced here: 42 us
  Pallas kernels  41.4 us (98%)
  between operations  0.64 us (2%)
    pallas_call x1, Pallas kernels, body(): pl.pallas_call(exchange, out_shape=(pltpu.VMEM(shape, jnp.float32), pltpu...  39.4 us
    pallas_call x1, Pallas kernels, body(): pl.pallas_call(put_out, out_shape=(jax.ShapeDtypeStruct(shape, jnp.float3...  2.03 us

profile of v2, /device:TPU:1, one launch (start us, length us, event | category | flops | bytes accessed | tf_op | source)
XLA Modules:
  0.0 42.0 jit_solution(8310289588830067813)
XLA Ops:
  0.6 39.4 %exchange.1 = (f32[16,256,128]{2,1,0:T(8,128)S(1)}, f32[16,256,128]{2,1,0:T(8,128)S(1)}) custom-call(f32[16,256,128]{2,1,0:T(8,128)} %bitcast.5, f32[16,256,128]{2,1,0:T(8,128)} %bitcast.6, f32[16,256,128]{2,1,0:T(8,128)} %bitcast.7), custom_call_target="tpu_custom_call" | custom-call | tf_op jit(solution)/shard_map/exchange/pallas_call | solution.py:219
  40.0 2.0 %put_out.1 = (f32[16,256,128]{2,1,0:T(8,128)}, f32[16,256,128]{2,1,0:T(8,128)}) custom-call(f32[16,256,128]{2,1,0:T(8,128)S(1)} %get-tuple-element.6.upd, f32[16,256,128]{2,1,0:T(8,128)S(1)} %get-tuple-element.7.new_w), custom_call_target="tpu_custom_call" | custom-call | tf_op jit(solution)/shard_map/put_out/pallas_call | solution.py:244

commit v3 on v2

--- a/solution.py
+++ b/solution.py
@@ -10,9 +10,10 @@
 MESH = pl.DeviceIdType.MESH
 LANES = 128
 N = 16
-CHUNKS = (64, 64, 64, 64)
-NEARS = 2
+CHUNKS = (80, 64, 64, 48)
+NEARS = 1
 ROUTES = "xyyY"
+GROUPS = (1, 1, 1, 4, 6, 3)
 STEP = 128
 SORT8 = (
     ((0, 2), (1, 3), (4, 6), (5, 7)),
@@ -43,7 +44,7 @@
 
 
 def exchange(m_ref, g_ref, w_ref, upd, new_w, m_buf, g_buf, w_buf, recv,
-             round_sem, load_sem, w_sem, out_sem, in_sem, near_sem, far_sem, core_sem, gather_sem):
+             round_sem, load_sem, out_sem, in_sem, near_sem, far_sem, core_sem, gather_sem):
     me = lax.axis_index("worker")
     x, y, c = me // 8, (me // 2) % 4, me % 2
 
@@ -74,22 +75,17 @@
     for o in near:
         signal(barrier, o)
     order = near + middle + last + [(0, 0, 0)]
-    loads = []
+    group = [g for g, blocks in enumerate(GROUPS) for _ in range(blocks)]
     for i, o in enumerate(order):
-        block = at(*o)
-        pair = (
-            pltpu.make_async_copy(m_ref.at[block], m_buf.at[block], load_sem.at[0, i]),
-            pltpu.make_async_copy(g_ref.at[block], g_buf.at[block], load_sem.at[1, i]),
-        )
-        for copy in pair:
-            copy.start()
-        loads.append(pair)
-    w_load = pltpu.make_async_copy(w_ref.at[me], w_buf, w_sem)
-    w_load.start()
+        block, sem = at(*o), load_sem.at[group[i]]
+        pltpu.make_async_copy(m_ref.at[block], m_buf.at[block], sem).start()
+        pltpu.make_async_copy(g_ref.at[block], g_buf.at[block], sem).start()
+    pltpu.make_async_copy(w_ref.at[me], w_buf, load_sem.at[group[-1]]).start()
 
     def update(i):
-        for copy in loads[i]:
-            copy.wait()
+        if i == 0 or group[i] != group[i - 1]:
+            copies = 2 * GROUPS[group[i]] + (group[i] == group[-1])
+            wait_bytes(m_buf.at[pl.ds(0, copies)], load_sem.at[group[i]])
         block = at(*order[i])
 
         def one(r, _):
@@ -136,15 +132,15 @@
         return 0
 
     lax.fori_loop(0, upd.shape[1] // 32, own, 0)
-    w_load.wait()
 
     other_core, other_x = at(0, 0, 1), at(1, 0, 0)
-
-    sides = ((1, 1), (2, 3))
 
     def gather(block, k, r_sem, peer):
         part = new_w.at[block, spans[k]]
         send(part, part, gather_sem, r_sem, peer)
+
+    def wait_blocks(blocks, k, sem):
+        wait_bytes(new_w.at[pl.ds(0, blocks), spans[k]], sem)
 
     def select(k):
         wait_bytes(recv.at[pl.ds(0, N - 1), spans[k]], in_sem.at[k])
@@ -156,39 +152,31 @@
             return 0
 
         lax.fori_loop(0, CHUNKS[k] // 8, one, 0)
-        gather(me, k, near_sem.at[k, 3], at(0, 2, 0))
-        for i, dy in sides:
-            gather(me, k, near_sem.at[k, i], at(0, dy, 0))
+        for dy in (2, 1, 3):
+            gather(me, k, near_sem.at[k, 1], at(0, dy, 0))
         gather(me, k, near_sem.at[k, 0], other_x)
         gather(me, k, core_sem, other_core)
 
     def relay(k):
-        wait_bytes(new_w.at[other_x, spans[k]], near_sem.at[k, 0])
+        wait_blocks(1, k, near_sem.at[k, 0])
         if ROUTES[k] != "x":
-            for i, dy in sides:
-                gather(other_x, k, far_sem.at[k, i], at(0, dy, 0))
+            for dy in (1, 3):
+                gather(other_x, k, far_sem.at[k], at(0, dy, 0))
                 if ROUTES[k] == "Y":
                     gather(other_x, k, core_sem, at(0, dy, 1))
         gather(other_x, k, core_sem, other_core)
-        for i, dy in sides:
-            block = at(0, -dy, 0)
-            wait_bytes(new_w.at[block, spans[k]], near_sem.at[k, i])
-            if ROUTES[k] == "x":
-                gather(block, k, far_sem.at[k, i], other_x)
-            gather(block, k, core_sem, other_core)
-        block = at(0, 2, 0)
-        wait_bytes(new_w.at[block, spans[k]], near_sem.at[k, 3])
-        gather(block, k, far_sem.at[k, 0], other_x)
-        if ROUTES[k] == "Y":
-            gather(block, k, core_sem, at(1, 0, 1))
-        gather(block, k, core_sem, other_core)
+        wait_blocks(3, k, near_sem.at[k, 1])
+        for dy in (2, 1, 3) if ROUTES[k] == "x" else (2,):
+            gather(at(0, dy, 0), k, far_sem.at[k], other_x)
+            if ROUTES[k] == "Y":
+                gather(at(0, dy, 0), k, core_sem, at(1, 0, 1))
+        for dy in (2, 1, 3):
+            gather(at(0, dy, 0), k, core_sem, other_core)
 
     def relay_far(k):
-        for i, dy in (*sides, (0, 2)):
-            block = at(1, -dy, 0)
-            wait_bytes(new_w.at[block, spans[k]], far_sem.at[k, i])
-            if ROUTES[k] != "Y":
-                gather(block, k, core_sem, other_core)
+        wait_blocks(3, k, far_sem.at[k])
+        for dy in (2, 1, 3) if ROUTES[k] != "Y" else ():
+            gather(at(1, dy, 0), k, core_sem, other_core)
 
     for step in (select, relay, relay_far):
         for k in every:
@@ -227,12 +215,11 @@
             pltpu.VMEM(shape[1:], jnp.float32),
             pltpu.VMEM(shape, jnp.float32),
             pltpu.SemaphoreType.REGULAR((2,)),
-            pltpu.SemaphoreType.DMA((2, N)),
-            pltpu.SemaphoreType.DMA,
+            pltpu.SemaphoreType.DMA((len(GROUPS),)),
             pltpu.SemaphoreType.DMA,
             pltpu.SemaphoreType.DMA((k,)),
-            pltpu.SemaphoreType.DMA((k, 4)),
-            pltpu.SemaphoreType.DMA((k, 3)),
+            pltpu.SemaphoreType.DMA((k, 2)),
+            pltpu.SemaphoreType.DMA((k,)),
             pltpu.SemaphoreType.DMA,
             pltpu.SemaphoreType.DMA,
         ],

time: 42.1 us -> 41.9 us (level)
  no operation moved by 1% of the time
where the time goes in v3:
time: 41.9 us; the launch traced here: 41.8 us
  Pallas kernels  41.1 us (98%)
  between operations  0.64 us (2%)
    pallas_call x1, Pallas kernels, body(): pl.pallas_call(exchange, out_shape=(pltpu.VMEM(shape, jnp.float32), pltpu...  39.1 us
    pallas_call x1, Pallas kernels, body(): pl.pallas_call(put_out, out_shape=(jax.ShapeDtypeStruct(shape, jnp.float3...  2.03 us

profile of v3, /device:TPU:1, one launch (start us, length us, event | category | flops | bytes accessed | tf_op | source)
XLA Modules:
  0.0 41.8 jit_solution(3923949267767850006)
XLA Ops:
  0.6 39.1 %exchange.1 = (f32[16,256,128]{2,1,0:T(8,128)S(1)}, f32[16,256,128]{2,1,0:T(8,128)S(1)}) custom-call(f32[16,256,128]{2,1,0:T(8,128)} %bitcast.5, f32[16,256,128]{2,1,0:T(8,128)} %bitcast.6, f32[16,256,128]{2,1,0:T(8,128)} %bitcast.7), custom_call_target="tpu_custom_call" | custom-call | tf_op jit(solution)/shard_map/exchange/pallas_call | solution.py:207
  39.7 2.0 %put_out.1 = (f32[16,256,128]{2,1,0:T(8,128)}, f32[16,256,128]{2,1,0:T(8,128)}) custom-call(f32[16,256,128]{2,1,0:T(8,128)S(1)} %get-tuple-element.6.upd, f32[16,256,128]{2,1,0:T(8,128)S(1)} %get-tuple-element.7.new_w), custom_call_target="tpu_custom_call" | custom-call | tf_op jit(solution)/shard_map/put_out/pallas_call | solution.py:231

commit v4 on v3

--- a/solution.py
+++ b/solution.py
@@ -60,8 +60,8 @@
             device_id={"worker": peer}, device_id_type=MESH,
         ).start()
 
-    near = [(1, 0, 0), (1, 0, 1), (0, 1, 0), (0, 3, 0), (0, 1, 1), (0, 3, 1), (0, 0, 1)]
-    middle = [(0, 2, 0), (0, 2, 1), (1, 1, 0), (1, 3, 0), (1, 1, 1), (1, 3, 1)]
+    near = [(1, 0, 0), (0, 1, 0), (0, 3, 0), (1, 0, 1), (0, 1, 1), (0, 3, 1), (0, 0, 1)]
+    middle = [(1, 1, 0), (1, 3, 0), (0, 2, 0), (0, 2, 1), (1, 1, 1), (1, 3, 1)]
     last = [(1, 2, 0), (1, 2, 1)]
     ring = [(1, 0, 0), (0, 1, 0), (0, 3, 0)]
     starts = [sum(CHUNKS[:k]) for k in range(len(CHUNKS))]
@@ -152,9 +152,9 @@
             return 0
 
         lax.fori_loop(0, CHUNKS[k] // 8, one, 0)
+        gather(me, k, near_sem.at[k, 0], other_x)
         for dy in (2, 1, 3):
             gather(me, k, near_sem.at[k, 1], at(0, dy, 0))
-        gather(me, k, near_sem.at[k, 0], other_x)
         gather(me, k, core_sem, other_core)
 
     def relay(k):

time: 41.9 us -> 41.9 us (level)
  no operation moved by 1% of the time
where the time goes in v4:
time: 41.9 us; the launch traced here: 41.8 us
  Pallas kernels  41.2 us (98%)
  between operations  0.64 us (2%)
    pallas_call x1, Pallas kernels, body(): pl.pallas_call(exchange, out_shape=(pltpu.VMEM(shape, jnp.float32), pltpu...  39.1 us
    pallas_call x1, Pallas kernels, body(): pl.pallas_call(put_out, out_shape=(jax.ShapeDtypeStruct(shape, jnp.float3...  2.03 us

profile of v4, /device:TPU:1, one launch (start us, length us, event | category | flops | bytes accessed | tf_op | source)
XLA Modules:
  0.0 41.8 jit_solution(8125880386686052203)
XLA Ops:
  0.6 39.1 %exchange.1 = (f32[16,256,128]{2,1,0:T(8,128)S(1)}, f32[16,256,128]{2,1,0:T(8,128)S(1)}) custom-call(f32[16,256,128]{2,1,0:T(8,128)} %bitcast.5, f32[16,256,128]{2,1,0:T(8,128)} %bitcast.6, f32[16,256,128]{2,1,0:T(8,128)} %bitcast.7), custom_call_target="tpu_custom_call" | custom-call | tf_op jit(solution)/shard_map/exchange/pallas_call | solution.py:207
  39.8 2.0 %put_out.1 = (f32[16,256,128]{2,1,0:T(8,128)}, f32[16,256,128]{2,1,0:T(8,128)}) custom-call(f32[16,256,128]{2,1,0:T(8,128)S(1)} %get-tuple-element.6.upd, f32[16,256,128]{2,1,0:T(8,128)S(1)} %get-tuple-element.7.new_w), custom_call_target="tpu_custom_call" | custom-call | tf_op jit(solution)/shard_map/put_out/pallas_call | solution.py:231
